TPU v7x, 512 devices: a whole 4x8x8 slice. The times are simulated.
512 devices in a mesh: dp: 64 (over y, z), tensor: 8 (over x, core).
Axes of the slice: x: 4, y: 8, z: 8, core: 2. Of those that a mesh axis runs over, the one named last changes fastest.
Arguments:
- activations: bfloat16 [81920, 5120], P('dp', 'tensor'), may hold values from -6 to 6
- cotangents: bfloat16 [81920, 1024], P('dp', 'tensor'), as said below
- error_old: bfloat16 [327680, 1024], P(('dp', 'tensor')), may hold values from -3 to 3
- pause_positions: int32 [320], replicated, may hold values from 0 to 1279, as said below
- initial_q: float32 [1024, 32], replicated, may hold values from -6 to 6
Outputs:
- error_new: bfloat16 [327680, 1024], P(('dp', 'tensor'))
- q_factor: float32 [1024, 32], P('tensor')
Inputs may be any that keep to these rules, and one draw needn't show every extreme that they name: pause_positions holds 320 different padding positions of a replica's batch, which attention masks out, in no particular order; they are the same for every replica. cotangents lie within 6 / sqrt(1280) in magnitude.
All inputs are finite; a program needn't handle non-finite values.
Results may differ from a plain program's by a relative error of at most 0.002.
Values may be sent and summed in bfloat16 or wider, within the bound.
No kernel may reach another device: no remote copies, remote signals or barrier semaphores. Data moves between devices by JAX's collectives and lax.ppermute only.
A program may use at most 64 MiB of HBM per device.

v0:
```python
import jax
import jax.numpy as jnp
from jax import lax
from jax.sharding import Mesh
from jax.sharding import PartitionSpec as P

TENSOR = ("tensor_0", "tensor_1")
DP_TENSOR = ("dp", "tensor_0", "tensor_1")


def from_everyone(x, axis):
    count = lax.axis_size(axis)
    return lax.all_to_all(jnp.broadcast_to(x[None], (count, *x.shape)), axis, 0, 0, tiled=True)


def laid_out(pieces, dim):
    dims = list(pieces.shape[1:])
    dims[dim] *= pieces.shape[0]
    return jnp.moveaxis(pieces, 0, dim).reshape(dims)


def whole_of(x, axes, dim):
    far, near = axes
    pieces = from_everyone(from_everyone(x, far), near)
    return laid_out(pieces.swapaxes(0, 1).reshape(-1, *x.shape), dim)


def padded_to(lines, count):
    spare = -len(lines) % count
    return jnp.pad(lines, [(0, spare)] + [(0, 0)] * (lines.ndim - 1))


def collect(x, axis, dim):
    return laid_out(from_everyone(x, axis), dim)


def in_blocks(x, dim, count):
    dims = x.shape
    pieces = x.reshape(*dims[:dim], count, dims[dim] // count, *dims[dim + 1 :])
    return jnp.moveaxis(pieces, dim, 0)


def summed_on_arrival(x, axis, dim):
    pieces = in_blocks(x, dim, lax.axis_size(axis))
    arrived = lax.all_to_all(pieces, axis, split_axis=0, concat_axis=0, tiled=True)
    return arrived.sum(axis=0)


def sum_by_parts(x, axes):
    lines = x.reshape(-1, x.shape[-1])
    padded = padded_to(lines, lax.axis_size(axes))
    whole = collect(summed_on_arrival(padded, axes, 0), axes, 0)
    return lax.slice_in_dim(whole, 0, len(lines)).reshape(x.shape)


def over_copies(x, axis):
    everything = from_everyone(x, axis)
    return jnp.sum(everything, axis=0)


def sent_and_summed(x, axis, dim):
    pieces = in_blocks(x, dim, lax.axis_size(axis))
    arrived = lax.all_to_all(pieces, axis, split_axis=0, concat_axis=0, tiled=True)
    return arrived.astype(jnp.float32).sum(axis=0)


def kept_mask(pause_positions, row_count):
    positions = jnp.arange(row_count, dtype=jnp.int32)
    struck = jnp.any(positions[:, None] == pause_positions[None, :], axis=1)
    return jnp.where(struck, 0, 1).astype(jnp.int32)


def body(activations, cotangents, error_old, pause_positions, initial_q):
    row_count = activations.shape[0]
    contract = (((0,), (0,)), ((), ()))
    kept = kept_mask(pause_positions, row_count)
    kept_count = row_count - pause_positions.shape[0]
    row_score = (1 - kept) * row_count + jnp.arange(row_count, dtype=jnp.int32)
    row_order = jnp.argsort(row_score)[:kept_count]
    features = jnp.take(activations, row_order, axis=0)
    cot_rows = jnp.take(cotangents, row_order, axis=0)
    gradient = lax.dot_general(
        features,
        whole_of(cot_rows, ("tensor_0", "tensor_1"), 1),
        contract,
        preferred_element_type=jnp.float32,
    )
    merged = gradient + error_old.astype(jnp.float32)
    replicas = lax.axis_size("dp")
    local_left = jnp.dot(merged, initial_q, precision=lax.Precision.HIGHEST)
    left_raw = sum_by_parts(local_left, "dp") / replicas
    gram = lax.dot_general(left_raw, left_raw, contract, precision=lax.Precision.HIGHEST)
    gram = over_copies(gram, TENSOR)
    factor_low = jnp.linalg.cholesky(gram)
    left_basis = lax.linalg.triangular_solve(
        factor_low, left_raw, left_side=False, lower=True, transpose_a=True
    )
    partial_q = lax.dot_general(merged, left_basis, contract, precision=lax.Precision.HIGHEST)
    own_q = sent_and_summed(partial_q.astype(jnp.bfloat16), TENSOR, 0)
    own_q = over_copies(own_q, "dp") / replicas
    q_full = collect(own_q, TENSOR, 0)
    update = jnp.dot(left_basis, q_full.T, precision=lax.Precision.HIGHEST)
    return ((merged - update).astype(jnp.bfloat16), own_q)


def solution(mesh):
    finer = Mesh(mesh.devices.reshape(mesh.shape["dp"], 4, 2), ("dp", "tensor_0", "tensor_1"))
    in_specs = (P("dp", TENSOR), P("dp", TENSOR), P(DP_TENSOR, None), P(), P())
    out_specs = (P(DP_TENSOR, None), P(TENSOR, None))
    return jax.shard_map(body, mesh=finer, in_specs=in_specs, out_specs=out_specs, check_vma=False)
```

profile of v0, /device:TPU:1, one launch (start us, length us, event | category | flops | bytes accessed | tf_op | source)
XLA Modules:
  0.0 168.8 jit_solution(12443346124636256609)
XLA Ops:
  0.6 1.1 fusion.3
  1.8 5.0 %sort.17 = (s32[1280]{0:T(1024)}, s32[1280]{0:T(1024)S(1)}) sort(s32[1280]{0:T(1024)S(1)} %iota_add_fusion, s32[1280]{0:T(1024)S(1)} %iota.37), dimensions={0}, to_apply=%region_1.2 | sort | flops 14080 | bytes 20480 | tf_op jit(solution)/shard_map/jit(argsort)/sort | solution.py:79
  6.8 4.0 %gather_fusion.1 = bf16[960,128]{1,0:T(8,128)(2,1)S(1)} fusion(bf16[1280,128]{1,0:T(8,128)(2,1)} %param.6, s32[1024]{0:T(1024)S(1)} %pad_clamp_fusion), kind=kCustom, calls=%fused_computation.1 | custom fusion | bytes 495360 | tf_op jit(solution)/shard_map/jit(_take)/gather | solution.py:81
  11.0 1.1 broadcast_in_dim.74
  12.1 4.8 %all-to-all-start = ((bf16[4,960,128]{2,1,0:T(8,128)(2,1)}), bf16[4,960,128]{2,1,0:T(8,128)(2,1)S(1)}, u32[]{:S(2)}, u32[]{:S(2)}) async-start(bf16[4,960,128]{2,1,0:T(8,128)(2,1)} %broadcast_in_dim.74), calls=%async_computation | async-start | bytes 1966080 | tf_op jit(solution)/shard_map/all_to_all | solution.py:13
  17.0 5.1 %gather_fusion = bf16[960,640]{1,0:T(8,128)(2,1)} fusion(bf16[1280,640]{1,0:T(8,128)(2,1)S(1)} %copy-done, s32[1024]{0:T(1024)S(1)} %pad_clamp_fusion), kind=kCustom, calls=%fused_computation | custom fusion | bytes 2461440 | tf_op jit(solution)/shard_map/jit(_take)/gather | solution.py:80
  22.1 4.3 %all-to-all-done = bf16[4,960,128]{2,1,0:T(8,128)(2,1)S(1)} async-done(((bf16[4,960,128]{2,1,0:T(8,128)(2,1)}), bf16[4,960,128]{2,1,0:T(8,128)(2,1)S(1)}, u32[]{:S(2)}, u32[]{:S(2)}) %all-to-all-start) | async-done | bytes 983072 | tf_op jit(solution)/shard_map/all_to_all | solution.py:13
  26.6 11.6 %all_to_all.40 = bf16[2,4,960,128]{3,2,1,0:T(8,128)(2,1)S(1)} all-to-all(bf16[2,4,960,128]{3,2,1,0:T(8,128)(2,1)S(1)} %broadcast_in_dim.75), channel_id=1, replica_groups=mesh['dp'=64,'tensor_0'=4,'tensor_1'=2] {'tensor_1'}, dimensions={0} | all-to-all | bytes 3932160 | tf_op jit(solution)/shard_map/all_to_all | solution.py:13
  38.3 1.2 copy-done.2
  39.5 0.4 copy-done.5
  39.9 1.7 convert_add_fusion
  41.6 1.5 copy-done.1
  43.1 2.2 %fusion.17 = f32[640,32]{1,0:T(8,128)S(1)} fusion(f32[640,1024]{1,0:T(8,128)S(1)} %convert_add_fusion, f32[1024,32]{0,1:T(8,128)S(1)} %copy-done.3), kind=kOutput, calls=%fused_computation.37 | convolution fusion | flops 251658240 | bytes 2834432 | tf_op jit(solution)/shard_map/dot_general | solution.py:90
  45.5 26.7 %all_to_all.41 = f32[64,1,320]{2,1,0:T(1,128)S(1)} all-to-all(f32[64,1,320]{2,1,0:T(1,128)S(1)} %reshape.81), channel_id=1, replica_groups=mesh['dp'=64,'tensor_0'=4,'tensor_1'=2] {'dp'}, dimensions={0} | all-to-all | bytes 163840 | tf_op jit(solution)/shard_map/all_to_all | solution.py:45
  72.2 0.5 broadcast.81
  72.7 0.9 reduce.6
  74.1 15.2 %all_to_all.42 = f32[64,1,320]{2,1,0:T(1,128)S(1)} all-to-all(f32[64,1,320]{2,1,0:T(1,128)S(1)} %reshape.83), channel_id=1, replica_groups=mesh['dp'=64,'tensor_0'=4,'tensor_1'=2] {'dp'}, dimensions={0} | all-to-all | bytes 163840 | tf_op jit(solution)/shard_map/all_to_all | solution.py:13
  89.3 0.9 reduce.7
  90.8 0.7 reshape.85
  91.5 6.1 %all-to-all-start.4 = ((f32[8,1,1024]{2,1,0:T(1,128)}), f32[8,1,1024]{2,1,0:T(1,128)S(1)}, u32[]{:S(2)}, u32[]{:S(2)}) async-start(f32[8,1,1024]{2,1,0:T(1,128)} %reshape.85), calls=%async_computation.4 | async-start | bytes 65536 | tf_op jit(solution)/shard_map/all_to_all | solution.py:13
  98.0 4.4 %all-to-all-done.4 = f32[8,1,1024]{2,1,0:T(1,128)S(1)} async-done(((f32[8,1,1024]{2,1,0:T(1,128)}), f32[8,1,1024]{2,1,0:T(1,128)S(1)}, u32[]{:S(2)}, u32[]{:S(2)}) %all-to-all-start.4) | async-done | bytes 32800 | tf_op jit(solution)/shard_map/all_to_all | solution.py:13
  102.3 0.7 reduce.8
  103.3 2.9 %cholesky.16 = f32[32,32]{1,0:T(8,128)S(1)} custom-call(f32[32,32]{1,0:T(8,128)S(1)} %fusion.15), custom_call_target="Cholesky" | custom-call | tf_op jit(solution)/shard_map/jit(cholesky)/cholesky | solution.py:94
  106.2 0.6 compare_reduce_fusion
  106.9 0.7 fusion.12
  107.5 2.4 %custom-call.6 = f32[1,32,32]{1,2,0:T(8,128)S(1)} custom-call(f32[1,32,32]{2,1,0:T(8,128)S(1)} %fusion.12), custom_call_target="InvertDiagBlocksLowerTriangular" | custom-call | tf_op jit(solution)/shard_map/triangular_solve | solution.py:95
  110.0 0.5 fusion.13
  110.5 3.4 %fusion.8 = bf16[4,8,8,128]{3,2,1,0:T(8,128)(2,1)S(1)} fusion(f32[640,1024]{1,0:T(8,128)} %copy-done.1, f32[640,32]{0,1:T(8,128)S(1)} %fusion.13), kind=kOutput, calls=%fused_computation.12 | convolution fusion | flops 251691008 | bytes 2768896 | tf_op jit(solution)/shard_map/dot_general | solution.py:98
  113.9 8.0 %all_to_all.43 = bf16[8,128,32]{1,2,0:T(8,128)(2,1)S(1)} all-to-all(bf16[8,128,32]{1,2,0:T(8,128)(2,1)S(1)} %bitcast.41), channel_id=1, replica_groups=mesh['dp'=64,'tensor_0'=4,'tensor_1'=2] {'tensor_0','tensor_1'}, dimensions={0} | all-to-all | bytes 131072 | tf_op jit(solution)/shard_map/all_to_all | solution.py:63
  122.0 30.8 %all_to_all.44 = f32[64,128,32]{1,2,0:T(8,128)S(1)} all-to-all(f32[64,128,32]{1,2,0:T(8,128)S(1)} %broadcast_in_dim.78), channel_id=1, replica_groups=mesh['dp'=64,'tensor_0'=4,'tensor_1'=2] {'dp'}, dimensions={0} | all-to-all | bytes 2097152 | tf_op jit(solution)/shard_map/all_to_all | solution.py:13
  152.9 10.8 %all_to_all.45 = f32[8,128,32]{1,2,0:T(8,128)S(1)} all-to-all(f32[8,128,32]{1,2,0:T(8,128)S(1)} %broadcast_in_dim.79), channel_id=1, replica_groups=mesh['dp'=64,'tensor_0'=4,'tensor_1'=2] {'tensor_0','tensor_1'}, dimensions={0} | all-to-all | bytes 262144 | tf_op jit(solution)/shard_map/all_to_all | solution.py:13
  163.8 5.1 %subtract_convert_fusion = bf16[640,1024]{1,0:T(8,128)(2,1)} fusion(f32[640,1024]{1,0:T(8,128)} %copy-done.1, f32[640,32]{0,1:T(8,128)S(1)} %fusion.13, f32[8,128,32]{1,2,0:T(8,128)S(1)} %all_to_all.45), kind=kOutput, calls=%fused_computation.2 | convolution fusion | flops 252968960 | bytes 4145152 | tf_op jit(solution)/shard_map/dot_general | solution.py:102
  (41 shorter events, 2.7 us)
Async XLA Ops:
  0.6 16.3 %copy-start = (bf16[1280,640]{1,0:T(8,128)(2,1)S(1)}, bf16[1280,640]{1,0:T(8,128)(2,1)}, u32[]{:S(2)}) copy-start(bf16[1280,640]{1,0:T(8,128)(2,1)} %param.5) | copy-start | bytes 4915204
  12.1 14.2 %all-to-all-start = ((bf16[4,960,128]{2,1,0:T(8,128)(2,1)}), bf16[4,960,128]{2,1,0:T(8,128)(2,1)S(1)}, u32[]{:S(2)}, u32[]{:S(2)}) async-start(bf16[4,960,128]{2,1,0:T(8,128)(2,1)} %broadcast_in_dim.74), calls=%async_computation | async-start | bytes 1966080 | tf_op jit(solution)/shard_map/all_to_all | solution.py:13
  38.2 1.3 copy-start.2
  38.2 1.7 copy-start.5
  39.9 3.2 %copy-start.3 = (f32[1024,32]{0,1:T(8,128)S(1)}, f32[1024,32]{0,1:T(8,128)}, u32[]{:S(2)}) copy-start(f32[1024,32]{0,1:T(8,128)} %param.9) | copy-start | bytes 393220
  41.6 1.5 copy-start.1
  91.5 10.8 %all-to-all-start.4 = ((f32[8,1,1024]{2,1,0:T(1,128)}), f32[8,1,1024]{2,1,0:T(1,128)S(1)}, u32[]{:S(2)}, u32[]{:S(2)}) async-start(f32[8,1,1024]{2,1,0:T(1,128)} %reshape.85), calls=%async_computation.4 | async-start | bytes 65536 | tf_op jit(solution)/shard_map/all_to_all | solution.py:13
  152.9 16.0 %copy-start.4 = (f32[128,32]{0,1:T(8,128)}, f32[128,32]{0,1:T(8,128)S(1)}, u32[]{:S(2)}) copy-start(f32[128,32]{0,1:T(8,128)S(1)} %broadcast_multiply_fusion.1) | copy-start | bytes 49156
where the time goes:
time: 170 us; the launch traced here: 169 us
  blocking collectives  103 us (61%)
  local copies, waits for them, and re-layouts  16.5 us (10%)
  other arithmetic  15.7 us (9%)
  matrix products  13.1 us (8%)
  starting transfers between devices  10.9 us (6%)
  waiting for transfers between devices  8.64 us (5%)
    all_to_all x4, blocking collectives, from_everyone(): lax.all_to_all(jnp.broadcast_to(x[None], (count, *x.shape)), axis, 0, 0,...  68.4 us
    all_to_all x1, blocking collectives, summed_on_arrival(): lax.all_to_all(pieces, axis, split_axis=0, concat_axis=0, tiled=True)  26.7 us
    all_to_all x2, starting transfers between devices, from_everyone(): lax.all_to_all(jnp.broadcast_to(x[None], (count, *x.shape)), axis, 0, 0,...  10.9 us
    all_to_all x2, waiting for transfers between devices, from_everyone(): lax.all_to_all(jnp.broadcast_to(x[None], (count, *x.shape)), axis, 0, 0,...  8.64 us
    all_to_all x1, blocking collectives, sent_and_summed(): lax.all_to_all(pieces, axis, split_axis=0, concat_axis=0, tiled=True)  7.95 us
    gather x1, local copies, waits for them, and re-layouts, body(): features = jnp.take(activations, row_order, axis=0)  5.14 us
    dot_general x1, matrix products, body(): update = jnp.dot(left_basis, q_full.T, precision=lax.Precision.HIGHEST)  5.08 us
    sort x1, other arithmetic, body(): row_order = jnp.argsort(row_score)[:kept_count]  5.04 us
  transfers between devices with their start and end apart: 2, of which 2 were waited for; matrix products, arithmetic and copies ran while one was open for 3% of the time, Pallas kernels for 0%

commit v1 on v0

v1 whole, which is shorter than its diff:
```python
import functools

import jax
import jax.numpy as jnp
from jax import lax
from jax.experimental import pallas as pl
from jax.experimental.pallas import tpu as pltpu
from jax.sharding import Mesh
from jax.sharding import PartitionSpec as P

DP = ("y", "z")
TENSOR = ("x", "c")
NEAR = ("z", "c")
FAR = ("y", "x")
CHUNK = 256
MIB = 1024 * 1024
F32 = jnp.float32
BF16 = jnp.bfloat16


def dot(a, b, contract, precision=None):
    return lax.dot_general(
        a, b, (contract, ((), ())), precision=precision, preferred_element_type=F32
    )


def params():
    return pltpu.CompilerParams(vmem_limit_bytes=24 * MIB)


def split(x):
    high = x.astype(BF16)
    return high, (x - high.astype(F32)).astype(BF16)


def selection(pauses, row_count, kept_count):
    count = pauses.shape[1]
    row = lax.broadcasted_iota(jnp.int32, (count, count), 0)
    col = lax.broadcasted_iota(jnp.int32, (count, count), 1)
    column = jnp.sum(
        jnp.where(row == col, pauses.astype(F32), 0.0), axis=1, keepdims=True
    )
    spot = lax.broadcasted_iota(jnp.int32, (1, row_count), 1).astype(F32)
    before = jnp.sum(jnp.where(column < spot, 1.0, 0.0), axis=0, keepdims=True)
    struck = jnp.sum(jnp.where(column == spot, 1.0, 0.0), axis=0, keepdims=True)
    target = jnp.where(struck > 0.0, -1.0, spot - before)
    rank = lax.broadcasted_iota(jnp.int32, (kept_count, row_count), 0).astype(F32)
    return jnp.where(rank == target, 1.0, 0.0).astype(BF16)


def compact_cotangents_kernel(pause_ref, cot_ref, out_ref):
    pick = selection(pause_ref[...], cot_ref.shape[0], out_ref.shape[1])
    kept = dot(pick, cot_ref[...], ((1,), (0,))).astype(BF16)
    for copy in range(out_ref.shape[0]):
        out_ref[copy] = kept


def compact_features_kernel(pause_ref, act_ref, out_ref, pick_ref):
    @pl.when(pl.program_id(0) == 0)
    def _():
        pick_ref[...] = selection(pause_ref[...], act_ref.shape[0], out_ref.shape[0])

    out_ref[...] = dot(pick_ref[...], act_ref[...], ((1,), (0,))).astype(BF16)


def merge_kernel(core_ref, feat_ref, own_ref, other_ref, err_ref, q_ref, merged_ref, left_ref, acc_ref):
    step = pl.program_id(0)
    first = core_ref[0] == 0
    own, other = own_ref[0], other_ref[0]
    low = jnp.where(first, own, other)
    high = jnp.where(first, other, own)
    cots = jnp.concatenate([low, high], axis=1)
    merged = dot(feat_ref[...], cots, ((0,), (0,))) + err_ref[...].astype(F32)
    merged_ref[...] = merged
    m_high, m_low = split(merged)
    q_high, q_low = split(q_ref[...])
    rank = q_high.shape[0]
    both = dot(jnp.concatenate([q_high, q_low], axis=0), m_high, ((1,), (1,)))
    part = both[:rank] + both[rank:] + dot(q_high, m_low, ((1,), (1,)))

    @pl.when(step == 0)
    def _():
        acc_ref[...] = part

    @pl.when(step > 0)
    def _():
        acc_ref[...] += part

    @pl.when(step == pl.num_programs(0) - 1)
    def _():
        total = acc_ref[...].astype(BF16)
        for copy in range(left_ref.shape[0]):
            left_ref[copy] = total


def add_copies_kernel(in_ref, out_ref):
    total = in_ref[0].astype(F32)
    for copy in range(1, in_ref.shape[0]):
        total += in_ref[copy].astype(F32)
    total = total.astype(out_ref.dtype)
    for copy in range(out_ref.shape[0]):
        out_ref[copy] = total


def project_kernel(replicas, in_ref, merged_ref, left_ref, out_ref, halves_ref):
    step = pl.program_id(0)
    last = pl.num_programs(0) - 1
    rank = left_ref.shape[0]

    @pl.when(step == 0)
    def _():
        total = in_ref[0].astype(F32)
        for copy in range(1, in_ref.shape[0]):
            total += in_ref[copy].astype(F32)
        total = total / replicas
        left_ref[...] = total
        high, low = split(total)
        halves_ref[:rank] = high
        halves_ref[rank:] = low

    @pl.when(step < last)
    def _():
        m_high, m_low = split(merged_ref[...])
        both = dot(halves_ref[...], m_high, ((1,), (0,)))
        part = both[:rank] + both[rank:] + dot(halves_ref[:rank], m_low, ((1,), (0,)))
        lines = out_ref.shape[1]
        for piece in range(out_ref.shape[0]):
            out_ref[piece] = part[piece * lines : (piece + 1) * lines]

    @pl.when(step == last)
    def _():
        left = left_ref[...]
        gram = dot(left, left, ((1,), (1,)), lax.Precision.HIGHEST)
        wide = jnp.concatenate([gram, jnp.zeros((rank, out_ref.shape[2] - rank), F32)], axis=1)
        lines = out_ref.shape[1]
        for piece in range(out_ref.shape[0]):
            out_ref[piece] = wide[piece * lines : (piece + 1) * lines]


def inverse_factor(gram):
    rank = gram.shape[0]
    row = lax.broadcasted_iota(jnp.int32, (rank, rank), 0)
    col = lax.broadcasted_iota(jnp.int32, (rank, rank), 1)
    table = jnp.concatenate([gram, jnp.where(row == col, 1.0, 0.0)], axis=1)
    line = lax.broadcasted_iota(jnp.int32, (rank, 1), 0)
    for k in range(rank):
        column = table[:, k : k + 1]
        pivot = table[k : k + 1, k : k + 1]
        weight = jnp.where(line > k, column / pivot, 0.0)
        table = table - weight * table[k : k + 1, :]
    diagonal = jnp.sum(jnp.where(row == col, table[:, :rank], 0.0), axis=1, keepdims=True)
    return table[:, rank:] / jnp.sqrt(diagonal)


def finish_kernel(replicas, place_ref, in_ref, left_ref, merged_ref, err_ref, own_ref, q_ref, lhs_ref, rhs_ref):
    step = pl.program_id(0)
    rank, width = q_ref.shape

    @pl.when(step == 0)
    def _():
        table = jnp.concatenate([in_ref[piece] for piece in range(in_ref.shape[0])], axis=0)
        table = table / replicas
        inverse = inverse_factor(table[:, width : width + rank])
        q_new = dot(inverse, table[:, :width], ((1,), (0,)), lax.Precision.HIGHEST)
        basis = dot(inverse, left_ref[...], ((1,), (0,)), lax.Precision.HIGHEST)
        q_ref[...] = q_new
        q_high, q_low = split(q_new)
        b_high, b_low = split(basis)
        lhs_ref[...] = jnp.concatenate([b_high, b_low, b_high], axis=0)
        rhs_ref[...] = jnp.concatenate([q_high, q_high, q_low], axis=0)
        lanes = own_ref.shape[1]
        start = pl.multiple_of(place_ref[0] * lanes, lanes)
        own_ref[...] = q_ref[:, pl.ds(start, lanes)]

    here = pl.multiple_of(step * CHUNK, CHUNK)
    update = dot(lhs_ref[...], rhs_ref[:, pl.ds(here, CHUNK)], ((0,), (0,)))
    err_ref[...] = (merged_ref[...] - update).astype(BF16)


def whole(shape):
    return pl.BlockSpec(shape, lambda *_: (0,) * len(shape))


def scalar():
    return pl.BlockSpec(memory_space=pltpu.SMEM)


def to_all(pieces, axes):
    return lax.all_to_all(pieces, axes, split_axis=0, concat_axis=0, tiled=True)


def add_copies(x, count, dtype):
    return pl.pallas_call(
        add_copies_kernel,
        out_shape=jax.ShapeDtypeStruct((count, *x.shape[1:]), dtype),
        compiler_params=params(),
        name="add_copies",
    )(x)


def body(activations, cotangents, error_old, pause_positions, initial_q):
    row_count, features = activations.shape
    lanes = cotangents.shape[1]
    width, rank = initial_q.shape
    kept_count = row_count - pause_positions.shape[0]
    replicas = lax.axis_size(DP)
    line_x, across = lax.axis_size("x"), lax.axis_size("z")
    near, far = lax.axis_size(NEAR), lax.axis_size(FAR)
    chunks = width // CHUNK
    core = lax.axis_index("c").astype(jnp.int32).reshape(1)
    place = lax.axis_index(TENSOR).astype(jnp.int32).reshape(1)
    pauses = pause_positions.reshape(1, -1)

    cot_copies = pl.pallas_call(
        compact_cotangents_kernel,
        out_shape=jax.ShapeDtypeStruct((line_x, kept_count, lanes), BF16),
        compiler_params=params(),
        name="compact_cotangents",
    )(pauses, cotangents)
    own = to_all(cot_copies, "x")
    halves = 5 if features % 640 == 0 else 1
    kept_features = pl.pallas_call(
        compact_features_kernel,
        grid=(halves,),
        in_specs=[
            whole(pauses.shape),
            pl.BlockSpec((row_count, features // halves), lambda i: (0, i)),
        ],
        out_specs=pl.BlockSpec((kept_count, features // halves), lambda i: (0, i)),
        out_shape=jax.ShapeDtypeStruct((kept_count, features), BF16),
        scratch_shapes=[pltpu.VMEM((kept_count, row_count), BF16)],
        compiler_params=params(),
        cost_estimate=pl.CostEstimate(
            flops=2 * kept_count * row_count * features,
            bytes_accessed=4 * row_count * features,
            transcendentals=0,
        ),
        name="compact_features",
    )(pauses, activations)
    cores = lax.axis_size("c")
    other = lax.ppermute(own, "c", [(i, cores - 1 - i) for i in range(cores)])

    merged, left_copies = pl.pallas_call(
        merge_kernel,
        grid=(chunks,),
        in_specs=[
            scalar(),
            whole((kept_count, features)),
            pl.BlockSpec((1, kept_count, lanes), lambda i: (i, 0, 0)),
            pl.BlockSpec((1, kept_count, lanes), lambda i: (i, 0, 0)),
            pl.BlockSpec((features, CHUNK), lambda i: (0, i)),
            pl.BlockSpec((rank, CHUNK), lambda i: (0, i)),
        ],
        out_specs=[
            pl.BlockSpec((features, CHUNK), lambda i: (0, i)),
            whole((across, rank, features)),
        ],
        out_shape=[
            jax.ShapeDtypeStruct((features, width), F32),
            jax.ShapeDtypeStruct((across, rank, features), BF16),
        ],
        scratch_shapes=[pltpu.VMEM((rank, features), F32)],
        compiler_params=params(),
        name="merge",
    )(core, kept_features, own, other, error_old, initial_q.T)

    left_copies = add_copies(to_all(left_copies, "z"), lax.axis_size("y"), BF16)
    left_copies = to_all(left_copies, "y")

    left, q_pieces = pl.pallas_call(
        functools.partial(project_kernel, replicas),
        grid=(chunks + 1,),
        in_specs=[
            whole(left_copies.shape),
            pl.BlockSpec((features, CHUNK), lambda i: (0, jnp.minimum(i, chunks - 1))),
        ],
        out_specs=[
            whole((rank, features)),
            pl.BlockSpec((near, rank // near, CHUNK), lambda i: (0, 0, i)),
        ],
        out_shape=[
            jax.ShapeDtypeStruct((rank, features), F32),
            jax.ShapeDtypeStruct((near, rank // near, width + CHUNK), F32),
        ],
        scratch_shapes=[pltpu.VMEM((2 * rank, features), BF16)],
        compiler_params=params(),
        name="project",
    )(left_copies, merged)

    q_pieces = add_copies(to_all(q_pieces, NEAR), far, F32)
    q_pieces = add_copies(to_all(q_pieces, FAR), near, F32)
    q_pieces = to_all(q_pieces, NEAR)

    error_new, own_q = pl.pallas_call(
        functools.partial(finish_kernel, replicas),
        grid=(chunks,),
        in_specs=[
            scalar(),
            whole(q_pieces.shape),
            whole((rank, features)),
            pl.BlockSpec((features, CHUNK), lambda i: (0, i)),
        ],
        out_specs=[
            pl.BlockSpec((features, CHUNK), lambda i: (0, i)),
            whole((rank, lanes)),
        ],
        out_shape=[
            jax.ShapeDtypeStruct((features, width), BF16),
            jax.ShapeDtypeStruct((rank, lanes), F32),
        ],
        scratch_shapes=[
            pltpu.VMEM((rank, width), F32),
            pltpu.VMEM((3 * rank, features), BF16),
            pltpu.VMEM((3 * rank, width), BF16),
        ],
        compiler_params=params(),
        name="finish",
    )(place, q_pieces, left, merged)
    return error_new, own_q.T


def solution(mesh, sizes=(8, 8, 4, 2)):
    finer = Mesh(mesh.devices.reshape(sizes), ("y", "z", "x", "c"))
    everyone = ("y", "z", "x", "c")
    in_specs = (P(DP, TENSOR), P(DP, TENSOR), P(everyone, None), P(), P())
    out_specs = (P(everyone, None), P(TENSOR, None))
    return jax.shard_map(
        body, mesh=finer, in_specs=in_specs, out_specs=out_specs, check_vma=False
    )
```

time: 170 us -> 135 us (0.79)
  Pallas kernels: 0 us -> 19 us
  other arithmetic: 15.7 us -> 0 us
  blocking collectives: 103 us -> 87.6 us
  matrix products: 13.1 us -> 0 us
  local copies, waits for them, and re-layouts: 16.5 us -> 6.43 us
    pallas_call x0 -> x8, Pallas kernels: none -> 19 us  [the longest x1 5.58 us: body(): pl.pallas_call(functools.partial(finish_kernel, replicas), grid=(chunks,)...]
    all_to_all x6 -> x5, blocking collectives: 103 us -> 87.6 us  [to_all(): return lax.all_to_all(pieces, axes, split_axis=0, concat_axis=0, tiled=True)]
    dot_general x5 -> x0, matrix products: 12.6 us -> none  [the longest x1 5.08 us: body(): update = jnp.dot(left_basis, q_full.T, precision=lax.Precision.HIGHEST)]
    gather x2 -> x0, local copies, waits for them, and re-layouts: 9.13 us -> none  [the longest x1 5.14 us: body(): features = jnp.take(activations, row_order, axis=0)]
    ppermute x0 -> x1, starting transfers between devices: none -> 7.66 us  [body(): other = lax.ppermute(own, 'c', [(i, cores - 1 - i) for i in range(cores)])]
    all_to_all x2 -> x1, starting transfers between devices: 10.9 us -> 3.74 us  [to_all(): return lax.all_to_all(pieces, axes, split_axis=0, concat_axis=0, tiled=True)]
    another operation x5 -> x0, other arithmetic: 6.68 us -> none  [the longest x3 3.6 us: body(): factor_low = jnp.linalg.cholesky(gram)]
    sort x1 -> x0, other arithmetic: 5.04 us -> none  [body(): row_order = jnp.argsort(row_score)[:kept_count]]
  transfers between devices with their start and end apart: 2 -> 2, of which waited for: 2 -> 1; matrix products, arithmetic and copies ran while one was open for 3% -> 0% of each run, Pallas kernels for 0% -> 4%
where the time goes in v1:
time: 135 us
  blocking collectives  87.6 us (65%)
  Pallas kernels  19 us (14%)
  starting transfers between devices  11.4 us (8%)
  waiting for transfers between devices  9.63 us (7%)
  local copies, waits for them, and re-layouts  6.43 us (5%)
    all_to_all x5, blocking collectives, to_all(): return lax.all_to_all(pieces, axes, split_axis=0, concat_axis=0, tiled=True)  87.6 us
    all_to_all x1, waiting for transfers between devices, to_all(): return lax.all_to_all(pieces, axes, split_axis=0, concat_axis=0, tiled=True)  9.62 us
    ppermute x1, starting transfers between devices, body(): other = lax.ppermute(own, 'c', [(i, cores - 1 - i) for i in range(cores)])  7.66 us
    unnamed x16, local copies, waits for them, and re-layouts  5.75 us
    pallas_call x1, Pallas kernels, body(): pl.pallas_call(functools.partial(finish_kernel, replicas), grid=(chunks,)...  5.58 us
    pallas_call x1, Pallas kernels, body(): pl.pallas_call(compact_features_kernel, grid=(halves,), in_specs=[whole(p...  5.51 us
    pallas_call x1, Pallas kernels, body(): pl.pallas_call(merge_kernel, grid=(chunks,), in_specs=[scalar(), whole((k...  4.43 us
    all_to_all x1, starting transfers between devices, to_all(): return lax.all_to_all(pieces, axes, split_axis=0, concat_axis=0, tiled=True)  3.74 us
  transfers between devices with their start and end apart: 2, of which 1 were waited for; matrix products, arithmetic and copies ran while one was open for 0% of the time, Pallas kernels for 4%

profile of v1, /device:TPU:1, one launch (start us, length us, event | category | flops | bytes accessed | tf_op | source)
XLA Modules:
  0.0 134.8 jit_solution(15402080229134838893)
XLA Ops:
  0.6 0.7 reshape.15.pause_ref
  1.3 0.0 copy-start.5
  1.3 1.0 copy-done.5
  2.3 1.2 compact_cotangents.1
  3.5 14.2 %all_to_all.30.own_ref = bf16[4,960,128]{2,1,0:T(8,128)(2,1)S(1)} all-to-all(bf16[4,960,128]{2,1,0:T(8,128)(2,1)S(1)} %compact_cotangents.1), channel_id=1, replica_groups=mesh['y'=8,'z'=8,'x'=4,'c'=2] {'x'}, dimensions={0} | all-to-all | bytes 1966080 | tf_op jit(solution)/shard_map/all_to_all | solution.py:189
  17.7 0.0 copy-start
  17.7 7.7 %collective-permute-start = (bf16[4,960,128]{2,1,0:T(8,128)(2,1)S(1)}, bf16[4,960,128]{2,1,0:T(8,128)(2,1)S(1)}, u32[]{:S(2)}, u32[]{:S(2)}) collective-permute-start(bf16[4,960,128]{2,1,0:T(8,128)(2,1)S(1)} %all_to_all.30.own_ref), channel_id=1, source_target_pairs={{0,1},{1,0},{2,3},{3,2},{4,5},{5,4},{6,7},{7,6},{8,9},{9,8},{10,11... | collective-permute-start | bytes 2949128 | tf_op jit(solution)/shard_map/ppermute | solution.py:241
  25.4 0.0 copy-start.7
  25.4 1.4 %copy-done.7 = bf16[1280,640]{1,0:T(8,128)(2,1)S(1)} copy-done((bf16[1280,640]{1,0:T(8,128)(2,1)S(1)}, bf16[1280,640]{1,0:T(8,128)(2,1)}, u32[]{:S(2)}) %copy-start.7) | copy-done | bytes 1638424
  26.8 0.0 copy-start.2
  26.8 0.0 copy-start.6
  26.8 5.5 %compact_features.1.feat_ref = bf16[960,640]{1,0:T(8,128)(2,1)S(1)} custom-call(s32[1,320]{1,0:T(1,128)S(1)} %reshape.15.pause_ref, bf16[1280,640]{1,0:T(8,128)(2,1)S(1)} %copy-done.7), custom_call_target="tpu_custom_call" | custom-call | flops 1572864000 | bytes 3276800 | tf_op jit(solution)/shard_map/compact_features/pallas_call | solution.py:222
  32.3 0.0 copy-done
  32.3 0.0 collective-permute-done.other_ref
  32.4 0.0 copy-start.3
  32.4 0.9 copy-done.3
  33.3 0.0 copy-done.2
  33.3 0.0 copy-done.6
  33.3 0.0 copy-start.1
  33.3 1.2 copy-done.1
  34.5 1.2 copy-done.4
  35.7 4.4 %merge.1 = (f32[640,1024]{1,0:T(8,128)S(1)}, bf16[8,32,640]{2,1,0:T(8,128)(2,1)S(1)}) custom-call(s32[1]{0:T(128)} %bitcast.1.core_ref, bf16[960,640]{1,0:T(8,128)(2,1)S(1)} %compact_features.1.feat_ref, bf16[4,960,128]{2,1,0:T(8,128)(2,1)S(1)} %copy-done.1, bf16[4,960,128]{2,1,0:T(8,128)(2,1)S(1)} %copy-done.4, bf16[640,1024]{1,0:T(8,128)(2,1)S(1)} %copy-done.2, ...), custom_call_target="tpu_custom_call" | custom-call | tf_op jit(solution)/shard_map/merge/pallas_call | solution.py:243
  40.1 23.6 %all_to_all.31.in_ref = bf16[8,32,640]{2,1,0:T(8,128)(2,1)S(1)} all-to-all(bf16[8,32,640]{2,1,0:T(8,128)(2,1)S(1)} %get-tuple-element.8), channel_id=1, replica_groups=mesh['y'=8,'z'=8,'x'=4,'c'=2] {'z'}, dimensions={0} | all-to-all | bytes 655360 | tf_op jit(solution)/shard_map/all_to_all | solution.py:189
  63.7 0.1 add_copies.3
  63.8 19.3 %all_to_all.32.in_ref = bf16[8,32,640]{2,1,0:T(8,128)(2,1)S(1)} all-to-all(bf16[8,32,640]{2,1,0:T(8,128)(2,1)S(1)} %add_copies.3), channel_id=1, replica_groups=mesh['y'=8,'z'=8,'x'=4,'c'=2] {'y'}, dimensions={0} | all-to-all | bytes 655360 | tf_op jit(solution)/shard_map/all_to_all | solution.py:189
  83.1 1.5 %project.1 = (f32[32,640]{1,0:T(8,128)S(1)}, f32[16,2,1280]{2,1,0:T(2,128)S(1)}) custom-call(bf16[8,32,640]{2,1,0:T(8,128)(2,1)S(1)} %all_to_all.32.in_ref, f32[640,1024]{1,0:T(8,128)S(1)} %get-tuple-element.9.merged_ref), custom_call_target="tpu_custom_call" | custom-call | tf_op jit(solution)/shard_map/project/pallas_call | solution.py:270
  84.6 13.6 %all_to_all.33.in_ref = f32[16,2,1280]{2,1,0:T(2,128)S(1)} all-to-all(f32[16,2,1280]{2,1,0:T(2,128)S(1)} %get-tuple-element.10), channel_id=1, replica_groups=mesh['y'=8,'z'=8,'x'=4,'c'=2] {'z','c'}, dimensions={0} | all-to-all | bytes 327680 | tf_op jit(solution)/shard_map/all_to_all | solution.py:189
  98.2 16.9 %all_to_all.34.in_ref = f32[32,2,1280]{2,1,0:T(2,128)S(1)} all-to-all(f32[32,2,1280]{2,1,0:T(2,128)S(1)} %add_copies.4), channel_id=1, replica_groups=mesh['y'=8,'z'=8,'x'=4,'c'=2] {'y','x'}, dimensions={0} | all-to-all | bytes 655360 | tf_op jit(solution)/shard_map/all_to_all | solution.py:189
  115.2 0.7 add_copies.5
  115.9 3.7 %all-to-all-start.5 = ((f32[16,2,1280]{2,1,0:T(2,128)}), f32[16,2,1280]{2,1,0:T(2,128)S(1)}, u32[]{:S(2)}, u32[]{:S(2)}) async-start(f32[16,2,1280]{2,1,0:T(2,128)} %add_copies.5), calls=%async_computation.5 | async-start | bytes 327680 | tf_op jit(solution)/shard_map/all_to_all | solution.py:189
  119.6 9.6 %all-to-all-done.5.in_ref = f32[16,2,1280]{2,1,0:T(2,128)S(1)} async-done(((f32[16,2,1280]{2,1,0:T(2,128)}), f32[16,2,1280]{2,1,0:T(2,128)S(1)}, u32[]{:S(2)}, u32[]{:S(2)}) %all-to-all-start.5) | async-done | bytes 163872 | tf_op jit(solution)/shard_map/all_to_all | solution.py:189
  129.2 5.6 %finish.1 = (bf16[640,1024]{1,0:T(8,128)(2,1)}, f32[32,128]{1,0:T(8,128)}) custom-call(s32[1]{0:T(128)} %bitcast.place_ref, f32[16,2,1280]{2,1,0:T(2,128)S(1)} %all-to-all-done.5.in_ref, f32[32,640]{1,0:T(8,128)S(1)} %get-tuple-element.11.left_ref, f32[640,1024]{1,0:T(8,128)S(1)} %get-tuple-element.9.merged_ref), custom_call_target="tpu_custom_call" | custom-call | tf_op jit(solution)/shard_map/finish/pallas_call | solution.py:294
  (2 shorter events, 0.0 us)
Async XLA Ops:
  1.3 1.0 copy-start.5
  17.7 14.6 %copy-start = (bf16[4,960,128]{2,1,0:T(8,128)(2,1)}, bf16[4,960,128]{2,1,0:T(8,128)(2,1)S(1)}, u32[]{:S(2)}) copy-start(bf16[4,960,128]{2,1,0:T(8,128)(2,1)S(1)} %all_to_all.30.own_ref) | copy-start | bytes 2949124
  17.7 14.6 %collective-permute-start = (bf16[4,960,128]{2,1,0:T(8,128)(2,1)S(1)}, bf16[4,960,128]{2,1,0:T(8,128)(2,1)S(1)}, u32[]{:S(2)}, u32[]{:S(2)}) collective-permute-start(bf16[4,960,128]{2,1,0:T(8,128)(2,1)S(1)} %all_to_all.30.own_ref), channel_id=1, source_target_pairs={{0,1},{1,0},{2,3},{3,2},{4,5},{5,4},{6,7},{7,6},{8,9},{9,8},{10,11... | collective-permute-start | bytes 2949128 | tf_op jit(solution)/shard_map/ppermute | solution.py:241
  25.4 1.4 %copy-start.7 = (bf16[1280,640]{1,0:T(8,128)(2,1)S(1)}, bf16[1280,640]{1,0:T(8,128)(2,1)}, u32[]{:S(2)}) copy-start(bf16[1280,640]{1,0:T(8,128)(2,1)} %act_ref.1) | copy-start | bytes 4915204
  26.8 6.5 %copy-start.2 = (bf16[640,1024]{1,0:T(8,128)(2,1)S(1)}, bf16[640,1024]{1,0:T(8,128)(2,1)}, u32[]{:S(2)}) copy-start(bf16[640,1024]{1,0:T(8,128)(2,1)} %err_ref.1) | copy-start | bytes 3932164
  26.8 6.5 %copy-start.6 = (f32[1024,32]{0,1:T(8,128)S(1)}, f32[1024,32]{0,1:T(8,128)}, u32[]{:S(2)}) copy-start(f32[1024,32]{0,1:T(8,128)} %param.9) | copy-start | bytes 393220
  32.4 0.9 copy-start.3
  33.3 1.2 copy-start.1
  34.5 1.2 copy-start.4
  115.9 13.4 %all-to-all-start.5 = ((f32[16,2,1280]{2,1,0:T(2,128)}), f32[16,2,1280]{2,1,0:T(2,128)S(1)}, u32[]{:S(2)}, u32[]{:S(2)}) async-start(f32[16,2,1280]{2,1,0:T(2,128)} %add_copies.5), calls=%async_computation.5 | async-start | bytes 327680 | tf_op jit(solution)/shard_map/all_to_all | solution.py:189
